TPU v7x, 128 devices: a whole 4x4x4 slice. The times are simulated.
128 devices in a mesh: side: 2 (over core), grp: 8 (over x_hi, y), tp: 8 (over x_lo, z).
Axes of the slice: x: 4 (x_hi: 2, x_lo: 2; x = x_hi * 2 + x_lo), y: 4, z: 4, core: 2. Of those that a mesh axis runs over, the one named last changes fastest.
Arguments:
- queries: bfloat16 [192, 4096], P('grp', 'side'), may hold values from -6 to 6
- kv_cache: bfloat16 [192, 16, 192, 256], P('grp', ('side', 'tp')), may hold values from -6 to 6
- lengths: int32 [192], P('grp'), may hold values from 2 to 768, as said below
- out_weight: bfloat16 [4096, 2048], P(('side', 'tp')), may hold values from -1 to 1
- resid: bfloat16 [192, 2048], P('grp'), may hold values from -6 to 6
- norm_gain: float32 [2048], replicated, may hold values from 0.1 to 1.9
- expert_ids: int32 [192, 8], P('grp'), may hold values from 0 to 127, all different within a row; in each aligned block of 24 rows (0 to 23, 24 to 47, ...) at most 3 rows name the same one
- expert_gates: float32 [192, 8], P('grp'), may hold values from 0.05 to 1
- w_gate_up: bfloat16 [128, 2048, 1536], P(('side', 'grp', 'tp')), may hold values from -0.125 to 0.125
- w_down: bfloat16 [128, 768, 2048], P(('side', 'grp', 'tp')), may hold values from -0.21875 to 0.21875
Outputs:
- layer_out: bfloat16 [192, 2048], P('grp', ('side', 'tp'))
Inputs may be any that keep to these rules, and one draw needn't show every extreme that they name: `lengths`: every row's cache holds at least two tokens; some row holds exactly 768. `expert_ids`: each row names 8 different experts. Among the rows of one row group no expert is named by more than 3 rows; in some group an expert is named by exactly 3.
All inputs are finite; a program needn't handle non-finite values.
Results may differ from a plain program's by a relative error of at most 0.017.
Values may be sent and summed in bfloat16 or wider, within the bound.
A program may use at most 64 MiB of HBM per device.

v0:
```python
import math
import jax
import jax.numpy as jnp
from jax import lax
from jax.sharding import PartitionSpec as P

QH = 32
KVH = 4
HD = 128
TOPK = 8


def swapped(value, axis, distance):
    mask = 2**distance
    pairs = [(source, source ^ mask) for source in range(lax.axis_size(axis))]
    return lax.ppermute(value, axis, pairs)


def body(
    queries,
    kv_cache,
    lengths,
    out_weight,
    resid,
    norm_gain,
    expert_ids,
    expert_gates,
    w_gate_up,
    w_down,
):
    lane_count = lax.axis_size("tp")
    tp_index = lax.axis_index("tp")
    side_count = lax.axis_size("side")
    section = lax.axis_index("side")
    grp_count = lax.axis_size("grp")
    group_size = side_count * lane_count
    member_index = section * lane_count + tp_index
    kv_parts = group_size // KVH
    group_heads = QH // KVH
    per_member = QH // group_size
    part_span = kv_cache.shape[2]
    model_width = out_weight.shape[1]
    piece_width = model_width // group_size
    rows_grp = lengths.shape[0]
    local_experts = w_gate_up.shape[0]
    experts_all = local_experts * side_count * grp_count * lane_count
    capacity = max(2, 2 * rows_grp * TOPK // experts_all)
    head_start = tp_index // kv_parts * group_heads * HD
    part_index = tp_index % kv_parts
    row_count = queries.shape[0]
    query_rows = lax.dynamic_slice_in_dim(queries, head_start, group_heads * HD, 1).reshape(
        row_count, group_heads, HD
    )
    key_rows = kv_cache[:, 0, :, :HD]
    value_rows = kv_cache[:, 0, :, HD:]
    positions = part_index * part_span + jnp.arange(part_span, dtype=jnp.int32)
    valid_mask = (positions[None, :] < lengths[:, None])[:, None, :]
    scores = jnp.einsum(
        "rgd,rpd->rgp", query_rows, key_rows, preferred_element_type=jnp.float32
    ) / math.sqrt(HD)
    scores = jnp.where(valid_mask, scores, -1e30)
    row_max = jnp.max(scores, axis=-1)
    for bit_index in range(kv_parts.bit_length() - 1):
        row_max = jnp.maximum(row_max, swapped(row_max, "tp", bit_index))
    weights = jnp.where(valid_mask, jnp.exp(scores - row_max[..., None]), 0.0)
    weight_sum = jnp.sum(weights, axis=-1)
    numerator = jnp.einsum(
        "rgp,rpd->rgd", weights.astype(jnp.bfloat16), value_rows, preferred_element_type=jnp.float32
    )
    for bit_index in range(kv_parts.bit_length() - 1):
        other_numerator, other_sum = swapped((numerator, weight_sum), "tp", bit_index)
        numerator = numerator + other_numerator
        weight_sum = weight_sum + other_sum
    heads_out = (numerator / weight_sum[..., None]).astype(jnp.bfloat16)
    mine = lax.dynamic_slice_in_dim(heads_out, part_index * per_member, per_member, 1).reshape(
        row_count, per_member * HD
    )
    projected = jnp.dot(mine, out_weight, preferred_element_type=jnp.float32)
    summed = lax.psum(projected, ("side", "tp"))
    middle = (resid.astype(jnp.float32) + summed).astype(jnp.bfloat16)
    middle_wide = middle.astype(jnp.float32)
    inv_rms = lax.rsqrt(jnp.mean(middle_wide * middle_wide, axis=-1, keepdims=True) + 1e-06)
    normed = (middle_wide * inv_rms * norm_gain).astype(jnp.bfloat16)
    column_experts = (
        (
            (section * grp_count + jnp.arange(grp_count, dtype=jnp.int32)[:, None]) * lane_count
            + tp_index
        )
        * local_experts
        + jnp.arange(local_experts, dtype=jnp.int32)[None, :]
    ).reshape(-1)
    matches = expert_ids[:, :, None] == column_experts[None, None, :]
    hit_count = jnp.sum(matches.astype(jnp.int32), axis=1)
    gate_cols = jnp.sum(jnp.where(matches, expert_gates[:, :, None], 0.0), axis=1)
    slot_rank = jnp.cumsum(hit_count, axis=0) - hit_count
    slot_ids = jnp.arange(capacity, dtype=jnp.int32)
    placed = (hit_count[:, :, None] == 1) & (slot_rank[:, :, None] == slot_ids[None, None, :])
    send_map = placed.astype(jnp.bfloat16)
    outgoing = jnp.einsum(
        "rcs,rd->csd", send_map, normed, preferred_element_type=jnp.float32
    ).astype(jnp.bfloat16)
    outgoing = outgoing.reshape(grp_count, local_experts, capacity, model_width)
    hidden = jnp.einsum(
        "gjcd,jdf->gjcf",
        lax.all_to_all(outgoing, "grp", split_axis=0, concat_axis=0, tiled=True),
        w_gate_up,
        preferred_element_type=jnp.float32,
    )
    inner_width = hidden.shape[-1] // 2
    activated = (jax.nn.silu(hidden[..., :inner_width]) * hidden[..., inner_width:]).astype(
        jnp.bfloat16
    )
    produced = jnp.einsum(
        "gjcf,jfd->gjcd", activated, w_down, preferred_element_type=jnp.float32
    ).astype(jnp.bfloat16)
    returned = lax.all_to_all(produced, "grp", split_axis=0, concat_axis=0, tiled=True)
    combine_weights = (send_map.astype(jnp.float32) * gate_cols[:, :, None]).reshape(row_count, -1)
    moe_part = jnp.dot(
        combine_weights,
        returned.reshape(-1, model_width).astype(jnp.float32),
        precision=lax.Precision.HIGHEST,
    )
    middle_mine = lax.dynamic_slice_in_dim(middle_wide, member_index * piece_width, piece_width, 1)
    moe_whole = lax.psum(moe_part, ("side", "tp"))
    return (
        middle_mine
        + lax.dynamic_slice_in_dim(moe_whole, member_index * piece_width, piece_width, 1)
    ).astype(jnp.bfloat16)


def solution(mesh):
    in_specs = (
        P("grp", "side"),
        P("grp", ("side", "tp"), None, None),
        P("grp"),
        P(("side", "tp"), None),
        P("grp", None),
        P(),
        P("grp", None),
        P("grp", None),
        P(("side", "grp", "tp"), None, None),
        P(("side", "grp", "tp"), None, None),
    )
    out_specs = P("grp", ("side", "tp"))
    return jax.shard_map(body, mesh=mesh, in_specs=in_specs, out_specs=out_specs, check_vma=False)
```

profile of v0, /device:TPU:1, one launch (start us, length us, event | category | flops | bytes accessed | tf_op | source)
XLA Modules:
  0.0 333.3 jit_solution(7118665528007655057)
XLA Ops:
  6.6 1.0 dynamic-slice_bitcast_fusion
  8.3 2.1 fusion.47
  10.3 2.5 collective-permute-start
  12.8 0.8 fusion.34
  13.9 3.4 %collective-permute-start.1 = (f32[24,8]{1,0:T(8,128)S(1)}, f32[24,8]{1,0:T(8,128)S(1)}, u32[]{:S(2)}, u32[]{:S(2)}) collective-permute-start(f32[24,8]{1,0:T(8,128)S(1)} %max.6), channel_id=1, source_target_pairs={{0,2},{1,3},{2,0},{3,1},{4,6},{5,7},{6,4},{7,5},{8,10},{9,11},{10,... | collective-permute-start | bytes 2312 | tf_op jit(solution)/shard_map/ppermute | solution.py:16
  18.7 1.0 collective-permute-start.4
  19.7 1.7 fusion.14
  22.0 2.9 collective-permute-start.5
  24.9 0.8 fusion.35
  25.9 1.1 collective-permute-done.5
  27.0 2.0 collective-permute-start.3
  29.1 2.9 collective-permute-done.3
  32.2 2.2 fusion.39
  34.4 1.3 convert_multiply_fusion
  35.7 130.8 %all-reduce.3.cloned.1.call-done = f32[24,2048]{1,0:T(8,128)} async-done(((f32[24,2048]{1,0:T(8,128)}), f32[24,2048]{1,0:T(8,128)}) %all-reduce.3.cloned.1.call-update) | async-done | bytes 196624 | tf_op jit(solution)/shard_map/psum | solution.py:79
  166.5 1.1 multiply_reduce_fusion
  167.5 0.9 fusion.10
  168.6 13.4 %all_to_all.10 = bf16[8,1,3,2048]{3,2,1,0:T(4,128)(2,1)S(1)} all-to-all(bf16[8,1,3,2048]{3,2,1,0:T(4,128)(2,1)S(1)} %copy.41), channel_id=1, replica_groups=mesh['side'=2,'grp'=8,'tp'=8] {'grp'}, dimensions={0} | all-to-all | bytes 196608 | tf_op jit(solution)/shard_map/all_to_all | solution.py:105
  182.0 3.7 %fusion.4 = f32[8,1,3,1536]{3,0,2,1:T(8,128)S(1)} fusion(bf16[1,2048,1536]{2,1,0:T(8,128)(2,1)} %param.18, bf16[8,1,3,2048]{3,2,1,0:T(4,128)(2,1)S(1)} %all_to_all.10), kind=kOutput, calls=%fused_computation.4 | convolution fusion | flops 150994944 | bytes 6537216 | tf_op jit(solution)/shard_map/gjcd,jdf->gjcf/dot_general | solution.py:103
  187.0 3.4 %all-to-all-start.1 = ((bf16[8,1,3,2048]{3,2,1,0:T(4,128)(2,1)}), bf16[8,1,3,2048]{3,2,1,0:T(4,128)(2,1)S(1)}, u32[]{:S(2)}, u32[]{:S(2)}) async-start(bf16[8,1,3,2048]{3,2,1,0:T(4,128)(2,1)} %copy.43), calls=%async_computation.1 | async-start | bytes 262144 | tf_op jit(solution)/shard_map/all_to_all | solution.py:116
  190.4 6.8 %all-to-all-done.1 = bf16[8,1,3,2048]{3,2,1,0:T(4,128)(2,1)S(1)} async-done(((bf16[8,1,3,2048]{3,2,1,0:T(4,128)(2,1)}), bf16[8,1,3,2048]{3,2,1,0:T(4,128)(2,1)S(1)}, u32[]{:S(2)}, u32[]{:S(2)}) %all-to-all-start.1) | async-done | bytes 98336 | tf_op jit(solution)/shard_map/all_to_all | solution.py:116
  197.9 1.9 fusion.48
  199.8 125.3 %all-reduce.5.cloned.1.call-done = f32[24,2048]{1,0:T(8,128)} async-done(((f32[24,2048]{1,0:T(8,128)}), f32[24,2048]{1,0:T(8,128)}) %all-reduce.5.cloned.1.call-update) | async-done | bytes 196624 | tf_op jit(solution)/shard_map/psum | solution.py:124
  325.1 1.3 add_convert_fusion.1
  (40 shorter events, 5.5 us)
Async XLA Ops:
  6.5 179.2 %copy-start = (bf16[1,768,2048]{2,1,0:T(8,128)(2,1)S(1)}, bf16[1,768,2048]{2,1,0:T(8,128)(2,1)}, u32[]{:S(2)}) copy-start(bf16[1,768,2048]{2,1,0:T(8,128)(2,1)} %param.19) | copy-start | bytes 9437188
  6.5 18.4 %copy-start.3 = (s32[24,8]{0,1:T(8,128)S(1)}, s32[24,8]{0,1:T(8,128)}, u32[]{:S(2)}) copy-start(s32[24,8]{0,1:T(8,128)} %param.16) | copy-start | bytes 2308
  6.5 159.9 %all-reduce.3.cloned.1.call-start = ((), (), s32[]{:S(2)}) async-start(), calls=%async_computation.2 | async-start | bytes 393216 | tf_op jit(solution)/shard_map/psum | solution.py:79
  8.3 158.2 %copy-start.1 = (bf16[24,2048]{1,0:T(8,128)(2,1)S(1)}, bf16[24,2048]{1,0:T(8,128)(2,1)}, u32[]{:S(2)}) copy-start(bf16[24,2048]{1,0:T(8,128)(2,1)} %param.14) | copy-start | bytes 294916
  10.3 3.6 %collective-permute-start = (f32[24,8]{1,0:T(8,128)S(1)}, f32[24,8]{1,0:T(8,128)S(1)}, u32[]{:S(2)}, u32[]{:S(2)}) collective-permute-start(f32[24,8]{1,0:T(8,128)S(1)} %get-tuple-element.9), channel_id=1, source_target_pairs={{0,1},{1,0},{2,3},{3,2},{4,5},{5,4},{6,7},{7,6},{8,9},{9,8},{10,11... | collective-permute-start | bytes 2312 | tf_op jit(solution)/shard_map/ppermute | solution.py:16
  13.9 4.6 %collective-permute-start.1 = (f32[24,8]{1,0:T(8,128)S(1)}, f32[24,8]{1,0:T(8,128)S(1)}, u32[]{:S(2)}, u32[]{:S(2)}) collective-permute-start(f32[24,8]{1,0:T(8,128)S(1)} %max.6), channel_id=1, source_target_pairs={{0,2},{1,3},{2,0},{3,1},{4,6},{5,7},{6,4},{7,5},{8,10},{9,11},{10,... | collective-permute-start | bytes 2312 | tf_op jit(solution)/shard_map/ppermute | solution.py:16
  18.7 3.3 collective-permute-start.4
  21.4 5.6 %collective-permute-start.2 = (f32[24,8,128]{2,1,0:T(8,128)S(1)}, f32[24,8,128]{2,1,0:T(8,128)S(1)}, u32[]{:S(2)}, u32[]{:S(2)}) collective-permute-start(f32[24,8,128]{2,1,0:T(8,128)S(1)} %fusion.14), channel_id=1, source_target_pairs={{0,1},{1,0},{2,3},{3,2},{4,5},{5,4},{6,7},{7,6},{8,9},{9,8},{10,11... | collective-permute-start | bytes 294920 | tf_op jit(solution)/shard_map/ppermute | solution.py:16
  22.0 5.0 %collective-permute-start.5 = (f32[24,8]{1,0:T(8,128)S(1)}, f32[24,8]{1,0:T(8,128)S(1)}, u32[]{:S(2)}, u32[]{:S(2)}) collective-permute-start(f32[24,8]{1,0:T(8,128)S(1)} %add.92), channel_id=1, source_target_pairs={{0,2},{1,3},{2,0},{3,1},{4,6},{5,7},{6,4},{7,5},{8,10},{9,11},{10,... | collective-permute-start | bytes 2312 | tf_op jit(solution)/shard_map/ppermute | solution.py:16
  27.0 5.1 %collective-permute-start.3 = (f32[24,8,128]{2,1,0:T(8,128)S(1)}, f32[24,8,128]{2,1,0:T(8,128)S(1)}, u32[]{:S(2)}, u32[]{:S(2)}) collective-permute-start(f32[24,8,128]{2,1,0:T(8,128)S(1)} %add.90), channel_id=1, source_target_pairs={{0,2},{1,3},{2,0},{3,1},{4,6},{5,7},{6,4},{7,5},{8,10},{9,11},{10,... | collective-permute-start | bytes 294920 | tf_op jit(solution)/shard_map/ppermute | solution.py:16
  185.7 4.7 %copy-start.2 = (f32[24,8,3]{0,2,1:T(4,128)S(1)}, f32[24,8,3]{0,2,1:T(4,128)}, u32[]{:S(2)}) copy-start(f32[24,8,3]{0,2,1:T(4,128)} %get-tuple-element.7) | copy-start | bytes 6916
  187.0 10.3 %all-to-all-start.1 = ((bf16[8,1,3,2048]{3,2,1,0:T(4,128)(2,1)}), bf16[8,1,3,2048]{3,2,1,0:T(4,128)(2,1)S(1)}, u32[]{:S(2)}, u32[]{:S(2)}) async-start(bf16[8,1,3,2048]{3,2,1,0:T(4,128)(2,1)} %copy.43), calls=%async_computation.1 | async-start | bytes 262144 | tf_op jit(solution)/shard_map/all_to_all | solution.py:116
  190.3 134.8 %all-reduce.5.cloned.1.call-start = ((), (), s32[]{:S(2)}) async-start(), calls=%async_computation.3 | async-start | bytes 393216 | tf_op jit(solution)/shard_map/psum | solution.py:124
Sparse Core Ops, SparseCore 0:
  34.5 131.9 all-reduce.2
  199.9 125.1 all-reduce.4
where the time goes:
time: 334 us; the launch traced here: 333 us
  waiting for transfers between devices  268 us (80%)
  starting transfers between devices  15.9 us (5%)
  between operations  13.5 us (4%)
  blocking collectives  13.4 us (4%)
  matrix products  13 us (4%)
  other arithmetic  6.89 us (2%)
    psum x1, waiting for transfers between devices, body(): summed = lax.psum(projected, ('side', 'tp'))  131 us
    psum x1, waiting for transfers between devices, body(): moe_whole = lax.psum(moe_part, ('side', 'tp'))  125 us
    all_to_all x1, blocking collectives, body(): lax.all_to_all(outgoing, 'grp', split_axis=0, concat_axis=0, tiled=True)  13.4 us
    ppermute x6, starting transfers between devices, swapped(): return lax.ppermute(value, axis, pairs)  12.4 us
    all_to_all x1, waiting for transfers between devices, body(): lax.all_to_all(produced, 'grp', split_axis=0, concat_axis=0, tiled=True)  6.8 us
  transfers between devices with their start and end apart: 9, of which 7 were waited for; matrix products, arithmetic and copies ran while one was open for 2% of the time, Pallas kernels for 0%

commit v1 on v0

--- a/solution.py
+++ b/solution.py
@@ -76,7 +76,7 @@
         row_count, per_member * HD
     )
     projected = jnp.dot(mine, out_weight, preferred_element_type=jnp.float32)
-    summed = lax.psum(projected, ("side", "tp"))
+    summed = lax.psum(lax.psum(projected, "side"), "tp")
     middle = (resid.astype(jnp.float32) + summed).astype(jnp.bfloat16)
     middle_wide = middle.astype(jnp.float32)
     inv_rms = lax.rsqrt(jnp.mean(middle_wide * middle_wide, axis=-1, keepdims=True) + 1e-06)

time: 334 us -> 307 us (0.919)
  waiting for transfers between devices: 268 us -> 244 us
    psum x1 -> x2, waiting for transfers between devices: 131 us -> 102 us  [body(): summed = lax.psum(lax.psum(projected, 'side'), 'tp')]
    psum x1, waiting for transfers between devices: 125 us -> 129 us  [body(): moe_whole = lax.psum(moe_part, ('side', 'tp'))]
  transfers between devices with their start and end apart: 9 -> 10, of which waited for: 7 -> 8; matrix products, arithmetic and copies ran while one was open for 2% -> 1% of each run, Pallas kernels for 0% -> 0%
where the time goes in v1:
time: 307 us
  waiting for transfers between devices  244 us (79%)
  starting transfers between devices  15.9 us (5%)
  between operations  13.2 us (4%)
  matrix products  13 us (4%)
  blocking collectives  12.9 us (4%)
  other arithmetic  4.98 us (2%)
    psum x1, waiting for transfers between devices, body(): moe_whole = lax.psum(moe_part, ('side', 'tp'))  129 us
    psum x2, waiting for transfers between devices, body(): summed = lax.psum(lax.psum(projected, 'side'), 'tp')  102 us
    all_to_all x1, blocking collectives, body(): lax.all_to_all(outgoing, 'grp', split_axis=0, concat_axis=0, tiled=True)  12.9 us
    ppermute x6, starting transfers between devices, swapped(): return lax.ppermute(value, axis, pairs)  12.4 us
    all_to_all x1, waiting for transfers between devices, body(): lax.all_to_all(produced, 'grp', split_axis=0, concat_axis=0, tiled=True)  6.8 us
    ppermute x6, waiting for transfers between devices, swapped(): return lax.ppermute(value, axis, pairs)  6.2 us
  transfers between devices with their start and end apart: 10, of which 8 were waited for; matrix products, arithmetic and copies ran while one was open for 1% of the time, Pallas kernels for 0%

profile of v1, /device:TPU:1, one launch (start us, length us, event | category | flops | bytes accessed | tf_op | source)
XLA Modules:
  0.0 306.9 jit_solution(7595563102747050186)
XLA Ops:
  6.6 1.0 dynamic-slice_bitcast_fusion
  8.3 2.1 fusion.47
  10.3 2.5 collective-permute-start
  12.8 1.1 collective-permute-done
  13.9 3.4 %collective-permute-start.1 = (f32[24,8]{1,0:T(8,128)S(1)}, f32[24,8]{1,0:T(8,128)S(1)}, u32[]{:S(2)}, u32[]{:S(2)}) collective-permute-start(f32[24,8]{1,0:T(8,128)S(1)} %max.6), channel_id=1, source_target_pairs={{0,2},{1,3},{2,0},{3,1},{4,6},{5,7},{6,4},{7,5},{8,10},{9,11},{10,... | collective-permute-start | bytes 2312 | tf_op jit(solution)/shard_map/ppermute | solution.py:16
  17.3 0.8 fusion.35
  18.7 1.0 collective-permute-start.4
  19.7 1.7 fusion.14
  22.0 2.9 collective-permute-start.5
  25.2 1.8 collective-permute-done.5
  27.0 2.0 collective-permute-start.3
  29.1 2.9 collective-permute-done.3
  32.2 2.2 fusion.39
  34.4 30.1 %all-reduce.4.cloned.1.call-done = f32[24,2048]{1,0:T(8,128)} async-done(((f32[24,2048]{1,0:T(8,128)}), f32[24,2048]{1,0:T(8,128)}) %all-reduce.4.cloned.1.call-update) | async-done | bytes 196624 | tf_op jit(solution)/shard_map/psum | solution.py:79
  65.2 71.6 %all-reduce.6.cloned.1.call-done = f32[24,2048]{1,0:T(8,128)} async-done(((f32[24,2048]{1,0:T(8,128)}), f32[24,2048]{1,0:T(8,128)}) %all-reduce.6.cloned.1.call-update) | async-done | bytes 196624 | tf_op jit(solution)/shard_map/psum | solution.py:79
  136.8 1.1 multiply_reduce_fusion
  137.9 0.9 fusion.10
  138.9 12.9 %all_to_all.10 = bf16[8,1,3,2048]{3,2,1,0:T(4,128)(2,1)S(1)} all-to-all(bf16[8,1,3,2048]{3,2,1,0:T(4,128)(2,1)S(1)} %copy.41), channel_id=1, replica_groups=mesh['side'=2,'grp'=8,'tp'=8] {'grp'}, dimensions={0} | all-to-all | bytes 196608 | tf_op jit(solution)/shard_map/all_to_all | solution.py:105
  151.8 3.7 %fusion.4 = f32[8,1,3,1536]{3,0,2,1:T(8,128)S(1)} fusion(bf16[1,2048,1536]{2,1,0:T(8,128)(2,1)} %param.18, bf16[8,1,3,2048]{3,2,1,0:T(4,128)(2,1)S(1)} %all_to_all.10), kind=kOutput, calls=%fused_computation.4 | convolution fusion | flops 150994944 | bytes 6537216 | tf_op jit(solution)/shard_map/gjcd,jdf->gjcf/dot_general | solution.py:103
  156.8 3.4 %all-to-all-start.1 = ((bf16[8,1,3,2048]{3,2,1,0:T(4,128)(2,1)}), bf16[8,1,3,2048]{3,2,1,0:T(4,128)(2,1)S(1)}, u32[]{:S(2)}, u32[]{:S(2)}) async-start(bf16[8,1,3,2048]{3,2,1,0:T(4,128)(2,1)} %copy.43), calls=%async_computation.1 | async-start | bytes 262144 | tf_op jit(solution)/shard_map/all_to_all | solution.py:116
  160.3 6.8 %all-to-all-done.1 = bf16[8,1,3,2048]{3,2,1,0:T(4,128)(2,1)S(1)} async-done(((bf16[8,1,3,2048]{3,2,1,0:T(4,128)(2,1)}), bf16[8,1,3,2048]{3,2,1,0:T(4,128)(2,1)S(1)}, u32[]{:S(2)}, u32[]{:S(2)}) %all-to-all-start.1) | async-done | bytes 98336 | tf_op jit(solution)/shard_map/all_to_all | solution.py:116
  167.8 1.9 fusion.48
  169.7 129.4 %all-reduce.8.cloned.1.call-done = f32[24,2048]{1,0:T(8,128)} async-done(((f32[24,2048]{1,0:T(8,128)}), f32[24,2048]{1,0:T(8,128)}) %all-reduce.8.cloned.1.call-update) | async-done | bytes 196624 | tf_op jit(solution)/shard_map/psum | solution.py:124
  299.1 1.3 add_convert_fusion.1
  (43 shorter events, 5.2 us)
Async XLA Ops:
  6.5 149.0 %copy-start = (bf16[1,768,2048]{2,1,0:T(8,128)(2,1)S(1)}, bf16[1,768,2048]{2,1,0:T(8,128)(2,1)}, u32[]{:S(2)}) copy-start(bf16[1,768,2048]{2,1,0:T(8,128)(2,1)} %param.19) | copy-start | bytes 9437188
  6.5 18.4 %copy-start.3 = (s32[24,8]{0,1:T(8,128)S(1)}, s32[24,8]{0,1:T(8,128)}, u32[]{:S(2)}) copy-start(s32[24,8]{0,1:T(8,128)} %param.16) | copy-start | bytes 2308
  6.5 58.0 %all-reduce.4.cloned.1.call-start = ((), (), s32[]{:S(2)}) async-start(), calls=%async_computation.2 | async-start | bytes 393216 | tf_op jit(solution)/shard_map/psum | solution.py:79
  10.3 126.5 %copy-start.1 = (bf16[24,2048]{1,0:T(8,128)(2,1)S(1)}, bf16[24,2048]{1,0:T(8,128)(2,1)}, u32[]{:S(2)}) copy-start(bf16[24,2048]{1,0:T(8,128)(2,1)} %param.14) | copy-start | bytes 294916
  10.3 3.6 %collective-permute-start = (f32[24,8]{1,0:T(8,128)S(1)}, f32[24,8]{1,0:T(8,128)S(1)}, u32[]{:S(2)}, u32[]{:S(2)}) collective-permute-start(f32[24,8]{1,0:T(8,128)S(1)} %get-tuple-element.9), channel_id=1, source_target_pairs={{0,1},{1,0},{2,3},{3,2},{4,5},{5,4},{6,7},{7,6},{8,9},{9,8},{10,11... | collective-permute-start | bytes 2312 | tf_op jit(solution)/shard_map/ppermute | solution.py:16
  13.9 4.6 %collective-permute-start.1 = (f32[24,8]{1,0:T(8,128)S(1)}, f32[24,8]{1,0:T(8,128)S(1)}, u32[]{:S(2)}, u32[]{:S(2)}) collective-permute-start(f32[24,8]{1,0:T(8,128)S(1)} %max.6), channel_id=1, source_target_pairs={{0,2},{1,3},{2,0},{3,1},{4,6},{5,7},{6,4},{7,5},{8,10},{9,11},{10,... | collective-permute-start | bytes 2312 | tf_op jit(solution)/shard_map/ppermute | solution.py:16
  18.7 3.3 %collective-permute-start.4 = (f32[24,8]{1,0:T(8,128)S(1)}, f32[24,8]{1,0:T(8,128)S(1)}, u32[]{:S(2)}, u32[]{:S(2)}) collective-permute-start(f32[24,8]{1,0:T(8,128)S(1)} %fusion.18), channel_id=1, source_target_pairs={{0,1},{1,0},{2,3},{3,2},{4,5},{5,4},{6,7},{7,6},{8,9},{9,8},{10,11... | collective-permute-start | bytes 2312 | tf_op jit(solution)/shard_map/ppermute | solution.py:16
  21.4 5.6 %collective-permute-start.2 = (f32[24,8,128]{2,1,0:T(8,128)S(1)}, f32[24,8,128]{2,1,0:T(8,128)S(1)}, u32[]{:S(2)}, u32[]{:S(2)}) collective-permute-start(f32[24,8,128]{2,1,0:T(8,128)S(1)} %fusion.14), channel_id=1, source_target_pairs={{0,1},{1,0},{2,3},{3,2},{4,5},{5,4},{6,7},{7,6},{8,9},{9,8},{10,11... | collective-permute-start | bytes 294920 | tf_op jit(solution)/shard_map/ppermute | solution.py:16
  22.0 5.0 %collective-permute-start.5 = (f32[24,8]{1,0:T(8,128)S(1)}, f32[24,8]{1,0:T(8,128)S(1)}, u32[]{:S(2)}, u32[]{:S(2)}) collective-permute-start(f32[24,8]{1,0:T(8,128)S(1)} %add.94), channel_id=1, source_target_pairs={{0,2},{1,3},{2,0},{3,1},{4,6},{5,7},{6,4},{7,5},{8,10},{9,11},{10,... | collective-permute-start | bytes 2312 | tf_op jit(solution)/shard_map/ppermute | solution.py:16
  27.0 5.1 %collective-permute-start.3 = (f32[24,8,128]{2,1,0:T(8,128)S(1)}, f32[24,8,128]{2,1,0:T(8,128)S(1)}, u32[]{:S(2)}, u32[]{:S(2)}) collective-permute-start(f32[24,8,128]{2,1,0:T(8,128)S(1)} %add.92), channel_id=1, source_target_pairs={{0,2},{1,3},{2,0},{3,1},{4,6},{5,7},{6,4},{7,5},{8,10},{9,11},{10,... | collective-permute-start | bytes 294920 | tf_op jit(solution)/shard_map/ppermute | solution.py:16
  34.4 102.5 %all-reduce.6.cloned.1.call-start = ((), (), s32[]{:S(2)}) async-start(), calls=%async_computation.3 | async-start | bytes 393216 | tf_op jit(solution)/shard_map/psum | solution.py:79
  155.5 4.7 %copy-start.2 = (f32[24,8,3]{0,2,1:T(4,128)S(1)}, f32[24,8,3]{0,2,1:T(4,128)}, u32[]{:S(2)}) copy-start(f32[24,8,3]{0,2,1:T(4,128)} %get-tuple-element.7) | copy-start | bytes 6916
  156.8 10.2 %all-to-all-start.1 = ((bf16[8,1,3,2048]{3,2,1,0:T(4,128)(2,1)}), bf16[8,1,3,2048]{3,2,1,0:T(4,128)(2,1)S(1)}, u32[]{:S(2)}, u32[]{:S(2)}) async-start(bf16[8,1,3,2048]{3,2,1,0:T(4,128)(2,1)} %copy.43), calls=%async_computation.1 | async-start | bytes 262144 | tf_op jit(solution)/shard_map/all_to_all | solution.py:116
  160.2 138.9 %all-reduce.8.cloned.1.call-start = ((), (), s32[]{:S(2)}) async-start(), calls=%async_computation.4 | async-start | bytes 393216 | tf_op jit(solution)/shard_map/psum | solution.py:124
Sparse Core Ops, SparseCore 0:
  34.5 30.0 all-reduce.3
  67.0 69.7 all-reduce.5
  169.8 129.2 all-reduce.7
